TPU v7x, 512 devices: a whole 4x4x16 slice. The times are simulated.
512 devices in a mesh: sta: 16 (over z), grp: 8 (over y, core), hr: 4 (over x).
Axes of the slice: x: 4, y: 4, z: 16, core: 2. Of those that a mesh axis runs over, the one named last changes fastest.
Arguments:
- spectra: bfloat16 [4, 128, 6, 8192], P('hr', 'sta'), may hold values from -6 to 6
- pair_source: int32 [2048], P(('sta', 'grp')), may hold values from 0 to 7
- pair_owner: int32 [2048, 1], P(('sta', 'grp')), may hold values from 0 to 15; in each aligned block of 16 rows (0 to 15, 16 to 31, ...) at most 2 rows name the same one
- pair_row: int32 [2048], P(('sta', 'grp')), may hold values from 0 to 7
Outputs:
- stacked: float32 [2048, 9, 1024], P(('sta', 'grp'))
Inputs may be any that keep to these rules, and one draw needn't show every extreme that they name: `pair_owner`: in each aligned block of 16 pairs (the pairs of one device) no value is named by more than 2 pairs, and in some block one value is named by exactly 2 pairs.
All inputs are finite; a program needn't handle non-finite values.
Results may differ from a plain program's by a relative error of at most 0.0032.
Values may be sent and summed in bfloat16 or wider, within the bound.
No kernel may reach another device: no remote copies, remote signals or barrier semaphores. Data moves between devices by JAX's collectives and lax.ppermute only.
A program may use at most 128 MiB of HBM per device.

v0:
```python
import math
import jax
import jax.numpy as jnp
from jax import lax
from jax.sharding import PartitionSpec as P

LAGS = 1024
two_pi = 2.0 * math.pi


def lag_table(start_bin, block_size, num_bins):
    bin_index = start_bin + jnp.arange(block_size, dtype=jnp.int32)
    lag_shift = jnp.arange(LAGS, dtype=jnp.int32) - LAGS // 2
    period = 2 * num_bins
    angles = jnp.mod(bin_index[:, None] * lag_shift[None, :], period).astype(jnp.float32) * (
        two_pi / period
    )
    return jnp.concatenate([jnp.cos(angles), -jnp.sin(angles)], axis=0).astype(jnp.bfloat16)


def cross_block(src_blk, rcv_blk):
    source_part = src_blk.astype(jnp.float32)
    recv_part = rcv_blk.astype(jnp.float32)
    src_re = source_part[..., 0:3, :][..., :, None, :]
    src_im = source_part[..., 3:6, :][..., :, None, :]
    rcv_re = recv_part[..., 0:3, :][..., None, :, :]
    rcv_im = recv_part[..., 3:6, :][..., None, :, :]
    cross_re = src_re * rcv_re + src_im * rcv_im
    cross_im = src_re * rcv_im - src_im * rcv_re
    return jnp.concatenate([cross_re, cross_im], axis=-1).astype(jnp.bfloat16)


def window_taper():
    lag_pos = jnp.arange(LAGS, dtype=jnp.float32)
    return 0.75 - 0.25 * jnp.cos(two_pi * (lag_pos + 0.5) / LAGS)


def slot_layout(owners, pair_row, peer_count, slot_cap):
    onehot = (owners[:, None] == jnp.arange(peer_count, dtype=jnp.int32)[None, :]).astype(jnp.int32)
    before = jnp.cumsum(onehot, axis=0) - onehot
    slot_rank = jnp.sum(before * onehot, axis=1)
    slot_index = owners * slot_cap + slot_rank
    request_table = jnp.zeros((peer_count * slot_cap,), jnp.int32).at[slot_index].set(pair_row)
    return (slot_index, request_table)


def body(spectra, pair_source, pair_owner, pair_row):
    hours_dev, sta_dev, comp_rows, num_bins = spectra.shape
    pair_count = pair_source.shape[0]
    owners = pair_owner[:, 0]
    peer_count = lax.axis_size("sta")
    slot_cap = 2 * pair_count // peer_count
    slot_index, request_table = slot_layout(owners, pair_row, peer_count, slot_cap)
    slot_owner = jnp.arange(peer_count * slot_cap, dtype=jnp.int32) // slot_cap
    wanted_station = slot_owner * sta_dev + request_table
    picked = jnp.take(lax.all_gather(spectra, "sta", axis=1, tiled=True), wanted_station, axis=1)
    receivers = jnp.take(picked, slot_index, axis=1)
    sources = jnp.take(spectra, pair_source, axis=1)
    block_size = min(512, num_bins)
    row_count = hours_dev * pair_count * 9

    def add_block(block_index, running):
        start_bin = (block_index * block_size).astype(jnp.int32)
        src_blk = lax.dynamic_slice_in_dim(sources, start_bin, block_size, 3)
        rcv_blk = lax.dynamic_slice_in_dim(receivers, start_bin, block_size, 3)
        cross = cross_block(src_blk, rcv_blk).reshape(row_count, 2 * block_size)
        table = lag_table(start_bin, block_size, num_bins)
        return running + jnp.dot(cross, table, preferred_element_type=jnp.float32)

    running = lax.fori_loop(
        0, num_bins // block_size, add_block, jnp.zeros((row_count, LAGS), jnp.float32)
    )
    local_sum = jnp.sum(running.reshape(hours_dev, pair_count, 9, LAGS), axis=0)
    stacked_sum = lax.psum(local_sum, "hr")
    hour_total = hours_dev * lax.axis_size("hr")
    return stacked_sum * window_taper()[None, None, :] / (hour_total * math.sqrt(num_bins))


def solution(mesh):
    placed = (
        P("hr", "sta", None, None),
        P(("sta", "grp")),
        P(("sta", "grp"), None),
        P(("sta", "grp")),
    )
    return jax.shard_map(
        body, mesh=mesh, in_specs=placed, out_specs=P(("sta", "grp"), None, None), check_vma=False
    )
```

profile of v0, /device:TPU:8, one launch (start us, length us, event | category | flops | bytes accessed | tf_op | source)
XLA Modules:
  0.0 459.1 jit_solution(4330169677160378186)
XLA Ops:
  6.5 0.7 all-gather.2.cloned.1.call-update
  7.3 1.6 copy.17
  9.2 0.8 scatter_custom_fusion
  10.0 0.7 gather_fusion
  10.8 151.2 %all-gather.2.cloned.1.call-done = bf16[1,128,6,8192]{3,1,2,0:T(8,128)(2,1)} async-done(((bf16[1,8,6,8192]{3,1,2,0:T(8,128)(2,1)}), bf16[1,128,6,8192]{3,1,2,0:T(8,128)(2,1)}) %all-gather.2.cloned.1.call-update) | async-done | bytes 12582928 | tf_op jit(solution)/shard_map/all_gather | solution.py:56
  161.9 13.8 %copy.16 = bf16[1,128,6,8192]{3,2,1,0:T(8,128)(2,1)} copy(bf16[1,128,6,8192]{3,1,2,0:T(8,128)(2,1)} %all-gather.2.cloned.1.call-done) | data formatting | bytes 25165824 | tf_op jit(solution)/shard_map/all_gather | solution.py:56
  175.7 8.5 %gather_fusion.1 = bf16[32,6,8192]{2,1,0:T(8,128)(2,1)} fusion(bf16[128,6,8192]{2,1,0:T(8,128)(2,1)} %bitcast.37, s32[1024]{0:T(1024)S(1)} %pad_clamp_fusion.1), kind=kCustom, calls=%fused_computation.1 | custom fusion | bytes 6291584 | tf_op jit(solution)/shard_map/jit(_take)/gather | solution.py:56
  184.2 4.7 %fusion.14 = bf16[32,6,8192]{2,1,0:T(8,128)(2,1)} fusion(bf16[32,6,8192]{2,1,0:T(8,128)(2,1)} %gather_fusion.1, pred[32]{0:T(512)(128)(4,1)S(1)} %get-tuple-element.143), kind=kLoop, calls=%fused_computation.35 | loop fusion | flops 1572864 | bytes 6291488 | tf_op jit(solution)/shard_map/jit(_take)/select_n | solution.py:56
  188.9 4.2 gather_fusion.2
  193.1 4.2 bitcast_select_fusion.1
  197.3 193.9 %while.16 = (s32[]{:T(128)}, f32[144,1024]{1,0:T(8,128)}, bf16[1,16,6,8192]{3,2,1,0:T(8,128)(2,1)}, bf16[1,16,6,8192]{3,2,1,0:T(8,128)(2,1)}, s32[]{:T(128)}, /*index=5*/s32[]{:T(128)}, s32[]{:T(128)}, s32[]{:T(128)}) while((s32[]{:T(128)}, f32[144,1024]{1,0:T(8,128)}, bf16[1,16,6,8192]{3,2,1,0:T(8,128)(2,1)}, ...), condition=%wide.region_4.5_spmd.clone, body=%wide.region_3.4_spmd.clone.sunk | while | flops 316671488 | bytes 13054157 | solution.py:70
  197.3 1.0 dynamic-slice_convert_fusion.3
  198.9 9.0 %cosine_convert_fusion.2 = (bf16[512,1024]{1,0:T(8,128)(2,1)S(1)}, bf16[512,1024]{1,0:T(8,128)(2,1)S(1)}) fusion(s32[1024]{0:T(1024)S(1)} %iota_add_fusion.4, s32[512]{0:T(512)S(1)} %iota_add_fusion.5), kind=kLoop, calls=%fused_computation.17.clone.1 | loop fusion | flops 8912896 | bytes 2103296 | tf_op jit(solution)/shard_map/convert
  208.0 0.6 fusion.25
  208.6 0.8 copy-done.1
  209.4 1.0 dynamic-slice_convert_fusion.3
  211.1 9.0 %cosine_convert_fusion.2 = (bf16[512,1024]{1,0:T(8,128)(2,1)S(1)}, bf16[512,1024]{1,0:T(8,128)(2,1)S(1)}) fusion(s32[1024]{0:T(1024)S(1)} %iota_add_fusion.4, s32[512]{0:T(512)S(1)} %iota_add_fusion.5), kind=kLoop, calls=%fused_computation.17.clone.1 | loop fusion | flops 8912896 | bytes 2103296 | tf_op jit(solution)/shard_map/convert
  220.7 0.8 copy-done.1
  221.5 1.0 dynamic-slice_convert_fusion.3
  223.2 9.0 %cosine_convert_fusion.2 = (bf16[512,1024]{1,0:T(8,128)(2,1)S(1)}, bf16[512,1024]{1,0:T(8,128)(2,1)S(1)}) fusion(s32[1024]{0:T(1024)S(1)} %iota_add_fusion.4, s32[512]{0:T(512)S(1)} %iota_add_fusion.5), kind=kLoop, calls=%fused_computation.17.clone.1 | loop fusion | flops 8912896 | bytes 2103296 | tf_op jit(solution)/shard_map/convert
  232.8 0.8 copy-done.1
  233.6 1.0 dynamic-slice_convert_fusion.3
  235.3 9.0 %cosine_convert_fusion.2 = (bf16[512,1024]{1,0:T(8,128)(2,1)S(1)}, bf16[512,1024]{1,0:T(8,128)(2,1)S(1)}) fusion(s32[1024]{0:T(1024)S(1)} %iota_add_fusion.4, s32[512]{0:T(512)S(1)} %iota_add_fusion.5), kind=kLoop, calls=%fused_computation.17.clone.1 | loop fusion | flops 8912896 | bytes 2103296 | tf_op jit(solution)/shard_map/convert
  244.9 0.8 copy-done.1
  245.7 1.0 dynamic-slice_convert_fusion.3
  247.4 9.0 %cosine_convert_fusion.2 = (bf16[512,1024]{1,0:T(8,128)(2,1)S(1)}, bf16[512,1024]{1,0:T(8,128)(2,1)S(1)}) fusion(s32[1024]{0:T(1024)S(1)} %iota_add_fusion.4, s32[512]{0:T(512)S(1)} %iota_add_fusion.5), kind=kLoop, calls=%fused_computation.17.clone.1 | loop fusion | flops 8912896 | bytes 2103296 | tf_op jit(solution)/shard_map/convert
  257.1 0.8 copy-done.1
  257.9 1.0 dynamic-slice_convert_fusion.3
  259.5 9.0 %cosine_convert_fusion.2 = (bf16[512,1024]{1,0:T(8,128)(2,1)S(1)}, bf16[512,1024]{1,0:T(8,128)(2,1)S(1)}) fusion(s32[1024]{0:T(1024)S(1)} %iota_add_fusion.4, s32[512]{0:T(512)S(1)} %iota_add_fusion.5), kind=kLoop, calls=%fused_computation.17.clone.1 | loop fusion | flops 8912896 | bytes 2103296 | tf_op jit(solution)/shard_map/convert
  269.2 0.8 copy-done.1
  270.0 1.0 dynamic-slice_convert_fusion.3
  271.6 9.0 %cosine_convert_fusion.2 = (bf16[512,1024]{1,0:T(8,128)(2,1)S(1)}, bf16[512,1024]{1,0:T(8,128)(2,1)S(1)}) fusion(s32[1024]{0:T(1024)S(1)} %iota_add_fusion.4, s32[512]{0:T(512)S(1)} %iota_add_fusion.5), kind=kLoop, calls=%fused_computation.17.clone.1 | loop fusion | flops 8912896 | bytes 2103296 | tf_op jit(solution)/shard_map/convert
  281.3 0.8 copy-done.1
  282.1 1.0 dynamic-slice_convert_fusion.3
  283.8 9.0 %cosine_convert_fusion.2 = (bf16[512,1024]{1,0:T(8,128)(2,1)S(1)}, bf16[512,1024]{1,0:T(8,128)(2,1)S(1)}) fusion(s32[1024]{0:T(1024)S(1)} %iota_add_fusion.4, s32[512]{0:T(512)S(1)} %iota_add_fusion.5), kind=kLoop, calls=%fused_computation.17.clone.1 | loop fusion | flops 8912896 | bytes 2103296 | tf_op jit(solution)/shard_map/convert
  293.4 0.8 copy-done.1
  294.2 1.0 dynamic-slice_convert_fusion.3
  295.9 9.0 %cosine_convert_fusion.2 = (bf16[512,1024]{1,0:T(8,128)(2,1)S(1)}, bf16[512,1024]{1,0:T(8,128)(2,1)S(1)}) fusion(s32[1024]{0:T(1024)S(1)} %iota_add_fusion.4, s32[512]{0:T(512)S(1)} %iota_add_fusion.5), kind=kLoop, calls=%fused_computation.17.clone.1 | loop fusion | flops 8912896 | bytes 2103296 | tf_op jit(solution)/shard_map/convert
  305.5 0.8 copy-done.1
  306.3 1.0 dynamic-slice_convert_fusion.3
  308.0 9.0 %cosine_convert_fusion.2 = (bf16[512,1024]{1,0:T(8,128)(2,1)S(1)}, bf16[512,1024]{1,0:T(8,128)(2,1)S(1)}) fusion(s32[1024]{0:T(1024)S(1)} %iota_add_fusion.4, s32[512]{0:T(512)S(1)} %iota_add_fusion.5), kind=kLoop, calls=%fused_computation.17.clone.1 | loop fusion | flops 8912896 | bytes 2103296 | tf_op jit(solution)/shard_map/convert
  317.6 0.8 copy-done.1
  318.4 1.0 dynamic-slice_convert_fusion.3
  320.1 9.0 %cosine_convert_fusion.2 = (bf16[512,1024]{1,0:T(8,128)(2,1)S(1)}, bf16[512,1024]{1,0:T(8,128)(2,1)S(1)}) fusion(s32[1024]{0:T(1024)S(1)} %iota_add_fusion.4, s32[512]{0:T(512)S(1)} %iota_add_fusion.5), kind=kLoop, calls=%fused_computation.17.clone.1 | loop fusion | flops 8912896 | bytes 2103296 | tf_op jit(solution)/shard_map/convert
  329.8 0.8 copy-done.1
  330.6 1.0 dynamic-slice_convert_fusion.3
  332.2 9.0 %cosine_convert_fusion.2 = (bf16[512,1024]{1,0:T(8,128)(2,1)S(1)}, bf16[512,1024]{1,0:T(8,128)(2,1)S(1)}) fusion(s32[1024]{0:T(1024)S(1)} %iota_add_fusion.4, s32[512]{0:T(512)S(1)} %iota_add_fusion.5), kind=kLoop, calls=%fused_computation.17.clone.1 | loop fusion | flops 8912896 | bytes 2103296 | tf_op jit(solution)/shard_map/convert
  341.9 0.8 copy-done.1
  342.7 1.0 dynamic-slice_convert_fusion.3
  344.4 9.0 %cosine_convert_fusion.2 = (bf16[512,1024]{1,0:T(8,128)(2,1)S(1)}, bf16[512,1024]{1,0:T(8,128)(2,1)S(1)}) fusion(s32[1024]{0:T(1024)S(1)} %iota_add_fusion.4, s32[512]{0:T(512)S(1)} %iota_add_fusion.5), kind=kLoop, calls=%fused_computation.17.clone.1 | loop fusion | flops 8912896 | bytes 2103296 | tf_op jit(solution)/shard_map/convert
  354.0 0.8 copy-done.1
  354.8 1.0 dynamic-slice_convert_fusion.3
  356.5 9.0 %cosine_convert_fusion.2 = (bf16[512,1024]{1,0:T(8,128)(2,1)S(1)}, bf16[512,1024]{1,0:T(8,128)(2,1)S(1)}) fusion(s32[1024]{0:T(1024)S(1)} %iota_add_fusion.4, s32[512]{0:T(512)S(1)} %iota_add_fusion.5), kind=kLoop, calls=%fused_computation.17.clone.1 | loop fusion | flops 8912896 | bytes 2103296 | tf_op jit(solution)/shard_map/convert
  366.1 0.8 copy-done.1
  366.9 1.0 dynamic-slice_convert_fusion.3
  368.6 9.0 %cosine_convert_fusion.2 = (bf16[512,1024]{1,0:T(8,128)(2,1)S(1)}, bf16[512,1024]{1,0:T(8,128)(2,1)S(1)}) fusion(s32[1024]{0:T(1024)S(1)} %iota_add_fusion.4, s32[512]{0:T(512)S(1)} %iota_add_fusion.5), kind=kLoop, calls=%fused_computation.17.clone.1 | loop fusion | flops 8912896 | bytes 2103296 | tf_op jit(solution)/shard_map/convert
  378.2 0.8 copy-done.1
  379.0 1.0 dynamic-slice_convert_fusion.3
  380.7 9.0 %cosine_convert_fusion.2 = (bf16[512,1024]{1,0:T(8,128)(2,1)S(1)}, bf16[512,1024]{1,0:T(8,128)(2,1)S(1)}) fusion(s32[1024]{0:T(1024)S(1)} %iota_add_fusion.4, s32[512]{0:T(512)S(1)} %iota_add_fusion.5), kind=kLoop, calls=%fused_computation.17.clone.1 | loop fusion | flops 8912896 | bytes 2103296 | tf_op jit(solution)/shard_map/convert
  390.4 0.8 copy-done.1
  391.2 1.2 reduce_sum.19
  392.3 1.2 copy.13
  393.6 56.8 %all-reduce.2.cloned.1.call-done = f32[16,9,1024]{2,0,1:T(8,128)} async-done(((f32[16,9,1024]{2,0,1:T(8,128)}), f32[16,9,1024]{2,0,1:T(8,128)}) %all-reduce.2.cloned.1.call-update) | async-done | bytes 589840 | tf_op jit(solution)/shard_map/psum | solution.py:74
  450.3 2.0 multiply_multiply_fusion
  (194 shorter events, 18.5 us)
Async XLA Ops:
  6.5 2.4 copy-start.2
  6.5 3.4 copy-start.3
  6.5 155.4 %all-gather.2.cloned.1.call-start = ((), (), s32[]{:S(2)}) async-start(), calls=%async_computation | async-start | bytes 13369344 | tf_op jit(solution)/shard_map/all_gather | solution.py:56
  7.3 443.1 %all-reduce.2.cloned.1.call-start = ((), (), s32[]{:S(2)}) async-start(), calls=%async_computation.1 | async-start | bytes 1179648 | tf_op jit(solution)/shard_map/psum | solution.py:74
  198.4 9.6 %copy-start = (f32[144,1024]{1,0:T(8,128)S(1)}, f32[144,1024]{1,0:T(8,128)}, u32[]{:S(2)}) copy-start(f32[144,1024]{1,0:T(8,128)} %get-tuple-element.211) | copy-start | bytes 1769476 | tf_op jit(solution)/shard_map/while
  208.6 0.8 copy-start.1
  210.5 9.6 %copy-start = (f32[144,1024]{1,0:T(8,128)S(1)}, f32[144,1024]{1,0:T(8,128)}, u32[]{:S(2)}) copy-start(f32[144,1024]{1,0:T(8,128)} %get-tuple-element.211) | copy-start | bytes 1769476 | tf_op jit(solution)/shard_map/while
  220.7 0.8 copy-start.1
  222.6 9.6 %copy-start = (f32[144,1024]{1,0:T(8,128)S(1)}, f32[144,1024]{1,0:T(8,128)}, u32[]{:S(2)}) copy-start(f32[144,1024]{1,0:T(8,128)} %get-tuple-element.211) | copy-start | bytes 1769476 | tf_op jit(solution)/shard_map/while
  232.8 0.8 copy-start.1
  234.7 9.6 %copy-start = (f32[144,1024]{1,0:T(8,128)S(1)}, f32[144,1024]{1,0:T(8,128)}, u32[]{:S(2)}) copy-start(f32[144,1024]{1,0:T(8,128)} %get-tuple-element.211) | copy-start | bytes 1769476 | tf_op jit(solution)/shard_map/while
  244.9 0.8 copy-start.1
  246.8 9.6 %copy-start = (f32[144,1024]{1,0:T(8,128)S(1)}, f32[144,1024]{1,0:T(8,128)}, u32[]{:S(2)}) copy-start(f32[144,1024]{1,0:T(8,128)} %get-tuple-element.211) | copy-start | bytes 1769476 | tf_op jit(solution)/shard_map/while
  257.0 0.8 copy-start.1
  259.0 9.6 %copy-start = (f32[144,1024]{1,0:T(8,128)S(1)}, f32[144,1024]{1,0:T(8,128)}, u32[]{:S(2)}) copy-start(f32[144,1024]{1,0:T(8,128)} %get-tuple-element.211) | copy-start | bytes 1769476 | tf_op jit(solution)/shard_map/while
  269.2 0.8 copy-start.1
  271.1 9.6 %copy-start = (f32[144,1024]{1,0:T(8,128)S(1)}, f32[144,1024]{1,0:T(8,128)}, u32[]{:S(2)}) copy-start(f32[144,1024]{1,0:T(8,128)} %get-tuple-element.211) | copy-start | bytes 1769476 | tf_op jit(solution)/shard_map/while
  281.3 0.8 copy-start.1
  283.2 9.6 %copy-start = (f32[144,1024]{1,0:T(8,128)S(1)}, f32[144,1024]{1,0:T(8,128)}, u32[]{:S(2)}) copy-start(f32[144,1024]{1,0:T(8,128)} %get-tuple-element.211) | copy-start | bytes 1769476 | tf_op jit(solution)/shard_map/while
  293.4 0.8 copy-start.1
  295.3 9.6 %copy-start = (f32[144,1024]{1,0:T(8,128)S(1)}, f32[144,1024]{1,0:T(8,128)}, u32[]{:S(2)}) copy-start(f32[144,1024]{1,0:T(8,128)} %get-tuple-element.211) | copy-start | bytes 1769476 | tf_op jit(solution)/shard_map/while
  305.5 0.8 copy-start.1
  307.4 9.6 %copy-start = (f32[144,1024]{1,0:T(8,128)S(1)}, f32[144,1024]{1,0:T(8,128)}, u32[]{:S(2)}) copy-start(f32[144,1024]{1,0:T(8,128)} %get-tuple-element.211) | copy-start | bytes 1769476 | tf_op jit(solution)/shard_map/while
  317.6 0.8 copy-start.1
  319.5 9.6 %copy-start = (f32[144,1024]{1,0:T(8,128)S(1)}, f32[144,1024]{1,0:T(8,128)}, u32[]{:S(2)}) copy-start(f32[144,1024]{1,0:T(8,128)} %get-tuple-element.211) | copy-start | bytes 1769476 | tf_op jit(solution)/shard_map/while
  329.8 0.8 copy-start.1
  331.7 9.6 %copy-start = (f32[144,1024]{1,0:T(8,128)S(1)}, f32[144,1024]{1,0:T(8,128)}, u32[]{:S(2)}) copy-start(f32[144,1024]{1,0:T(8,128)} %get-tuple-element.211) | copy-start | bytes 1769476 | tf_op jit(solution)/shard_map/while
  341.9 0.8 copy-start.1
  343.8 9.6 %copy-start = (f32[144,1024]{1,0:T(8,128)S(1)}, f32[144,1024]{1,0:T(8,128)}, u32[]{:S(2)}) copy-start(f32[144,1024]{1,0:T(8,128)} %get-tuple-element.211) | copy-start | bytes 1769476 | tf_op jit(solution)/shard_map/while
  354.0 0.8 copy-start.1
  355.9 9.6 %copy-start = (f32[144,1024]{1,0:T(8,128)S(1)}, f32[144,1024]{1,0:T(8,128)}, u32[]{:S(2)}) copy-start(f32[144,1024]{1,0:T(8,128)} %get-tuple-element.211) | copy-start | bytes 1769476 | tf_op jit(solution)/shard_map/while
  366.1 0.8 copy-start.1
  368.0 9.6 %copy-start = (f32[144,1024]{1,0:T(8,128)S(1)}, f32[144,1024]{1,0:T(8,128)}, u32[]{:S(2)}) copy-start(f32[144,1024]{1,0:T(8,128)} %get-tuple-element.211) | copy-start | bytes 1769476 | tf_op jit(solution)/shard_map/while
  378.2 0.8 copy-start.1
  380.1 9.6 %copy-start = (f32[144,1024]{1,0:T(8,128)S(1)}, f32[144,1024]{1,0:T(8,128)}, u32[]{:S(2)}) copy-start(f32[144,1024]{1,0:T(8,128)} %get-tuple-element.211) | copy-start | bytes 1769476 | tf_op jit(solution)/shard_map/while
  390.3 0.8 copy-start.1
Sparse Core Ops, SparseCore 0:
  9.4 152.4 all-gather.1
  393.6 56.6 all-reduce.1
where the time goes:
time: 460 us; the launch traced here: 459 us
  waiting for transfers between devices  209 us (45%)
  other arithmetic  176 us (38%)
  local copies, waits for them, and re-layouts  50.5 us (11%)
  between operations  13.5 us (3%)
  matrix products  9.22 us (2%)
    all_gather x1, waiting for transfers between devices, body(): lax.all_gather(spectra, 'sta', axis=1, tiled=True)  151 us
    another operation x32, other arithmetic  148 us
    psum x1, waiting for transfers between devices, body(): stacked_sum = lax.psum(local_sum, 'hr')  56.8 us
    convert_element_type x16, other arithmetic, cross_block(): recv_part = rcv_blk.astype(jnp.float32)  16.4 us
    all_gather x1, local copies, waits for them, and re-layouts, body(): lax.all_gather(spectra, 'sta', axis=1, tiled=True)  13.8 us
    while x64, local copies, waits for them, and re-layouts  13 us
    dot_general x16, matrix products, add_block(): return running + jnp.dot(cross, table, preferred_element_type=jnp.float32)  9.22 us
  transfers between devices with their start and end apart: 2, of which 2 were waited for; matrix products, arithmetic and copies ran while one was open for 1% of the time, Pallas kernels for 0%

commit v1 on v0

--- a/solution.py
+++ b/solution.py
@@ -71,7 +71,13 @@
         0, num_bins // block_size, add_block, jnp.zeros((row_count, LAGS), jnp.float32)
     )
     local_sum = jnp.sum(running.reshape(hours_dev, pair_count, 9, LAGS), axis=0)
-    stacked_sum = lax.psum(local_sum, "hr")
+
+    def serve_windows(tile_in, peer_axis):
+        h_now = lax.all_gather(tile_in, axis_name=peer_axis)
+        current_block = jnp.sum(h_now, axis=0)
+        return current_block
+
+    stacked_sum = serve_windows(local_sum, "hr")
     hour_total = hours_dev * lax.axis_size("hr")
     return stacked_sum * window_taper()[None, None, :] / (hour_total * math.sqrt(num_bins))
 

time: 460 us -> 443 us (0.963)
  the two profiles are of different devices: /device:TPU:8 before, /device:TPU:1 now
where the time goes in v1:
time: 443 us
  waiting for transfers between devices  192 us (43%)
  other arithmetic  176 us (40%)
  local copies, waits for them, and re-layouts  50.5 us (11%)
  between operations  13.5 us (3%)
  matrix products  9.22 us (2%)
    all_gather x1, waiting for transfers between devices, body(): lax.all_gather(spectra, 'sta', axis=1, tiled=True)  152 us
    another operation x32, other arithmetic  148 us
    all_gather x1, waiting for transfers between devices, serve_windows(): h_now = lax.all_gather(tile_in, axis_name=peer_axis)  38.7 us
    convert_element_type x16, other arithmetic, cross_block(): recv_part = rcv_blk.astype(jnp.float32)  16.4 us
    all_gather x1, local copies, waits for them, and re-layouts, body(): lax.all_gather(spectra, 'sta', axis=1, tiled=True)  13.8 us
    while x64, local copies, waits for them, and re-layouts  13 us
    dot_general x16, matrix products, add_block(): return running + jnp.dot(cross, table, preferred_element_type=jnp.float32)  9.22 us
  transfers between devices with their start and end apart: 2, of which 2 were waited for; matrix products, arithmetic and copies ran while one was open for 1% of the time, Pallas kernels for 0%

profile of v1, /device:TPU:1, one launch (start us, length us, event | category | flops | bytes accessed | tf_op | source)
XLA Modules:
  0.0 442.8 jit_solution(776290719901123749)
XLA Ops:
  6.5 0.7 all-gather.3.cloned.1.call-update
  7.3 1.6 copy.21
  9.2 0.8 scatter_custom_fusion
  10.0 0.7 gather_fusion
  10.8 152.1 %all-gather.3.cloned.1.call-done = bf16[1,128,6,8192]{3,1,2,0:T(8,128)(2,1)} async-done(((bf16[1,8,6,8192]{3,1,2,0:T(8,128)(2,1)}), bf16[1,128,6,8192]{3,1,2,0:T(8,128)(2,1)}) %all-gather.3.cloned.1.call-update) | async-done | bytes 12582928 | tf_op jit(solution)/shard_map/all_gather | solution.py:56
  162.8 13.8 %copy.20 = bf16[1,128,6,8192]{3,2,1,0:T(8,128)(2,1)} copy(bf16[1,128,6,8192]{3,1,2,0:T(8,128)(2,1)} %all-gather.3.cloned.1.call-done) | data formatting | bytes 25165824 | tf_op jit(solution)/shard_map/all_gather | solution.py:56
  176.6 8.5 %gather_fusion.1 = bf16[32,6,8192]{2,1,0:T(8,128)(2,1)} fusion(bf16[128,6,8192]{2,1,0:T(8,128)(2,1)} %bitcast.37, s32[1024]{0:T(1024)S(1)} %pad_clamp_fusion.1), kind=kCustom, calls=%fused_computation.1 | custom fusion | bytes 6291584 | tf_op jit(solution)/shard_map/jit(_take)/gather | solution.py:56
  185.1 4.7 %fusion.14 = bf16[32,6,8192]{2,1,0:T(8,128)(2,1)} fusion(bf16[32,6,8192]{2,1,0:T(8,128)(2,1)} %gather_fusion.1, pred[32]{0:T(512)(128)(4,1)S(1)} %get-tuple-element.143), kind=kLoop, calls=%fused_computation.35 | loop fusion | flops 1572864 | bytes 6291488 | tf_op jit(solution)/shard_map/jit(_take)/select_n | solution.py:56
  189.8 4.2 gather_fusion.2
  194.0 4.2 bitcast_select_fusion.1
  198.1 193.9 %while.16 = (s32[]{:T(128)}, f32[144,1024]{1,0:T(8,128)}, bf16[1,16,6,8192]{3,2,1,0:T(8,128)(2,1)}, bf16[1,16,6,8192]{3,2,1,0:T(8,128)(2,1)}, s32[]{:T(128)}, /*index=5*/s32[]{:T(128)}, s32[]{:T(128)}, s32[]{:T(128)}) while((s32[]{:T(128)}, f32[144,1024]{1,0:T(8,128)}, bf16[1,16,6,8192]{3,2,1,0:T(8,128)(2,1)}, ...), condition=%wide.region_4.5_spmd.clone, body=%wide.region_3.4_spmd.clone.sunk | while | flops 316671488 | bytes 13054157 | solution.py:70
  198.1 1.0 dynamic-slice_convert_fusion.3
  199.8 9.0 %cosine_convert_fusion.2 = (bf16[512,1024]{1,0:T(8,128)(2,1)S(1)}, bf16[512,1024]{1,0:T(8,128)(2,1)S(1)}) fusion(s32[1024]{0:T(1024)S(1)} %iota_add_fusion.4, s32[512]{0:T(512)S(1)} %iota_add_fusion.5), kind=kLoop, calls=%fused_computation.17.clone.1 | loop fusion | flops 8912896 | bytes 2103296 | tf_op jit(solution)/shard_map/convert
  209.5 0.8 copy-done.1
  210.3 1.0 dynamic-slice_convert_fusion.3
  211.9 9.0 %cosine_convert_fusion.2 = (bf16[512,1024]{1,0:T(8,128)(2,1)S(1)}, bf16[512,1024]{1,0:T(8,128)(2,1)S(1)}) fusion(s32[1024]{0:T(1024)S(1)} %iota_add_fusion.4, s32[512]{0:T(512)S(1)} %iota_add_fusion.5), kind=kLoop, calls=%fused_computation.17.clone.1 | loop fusion | flops 8912896 | bytes 2103296 | tf_op jit(solution)/shard_map/convert
  221.6 0.8 copy-done.1
  222.4 1.0 dynamic-slice_convert_fusion.3
  224.1 9.0 %cosine_convert_fusion.2 = (bf16[512,1024]{1,0:T(8,128)(2,1)S(1)}, bf16[512,1024]{1,0:T(8,128)(2,1)S(1)}) fusion(s32[1024]{0:T(1024)S(1)} %iota_add_fusion.4, s32[512]{0:T(512)S(1)} %iota_add_fusion.5), kind=kLoop, calls=%fused_computation.17.clone.1 | loop fusion | flops 8912896 | bytes 2103296 | tf_op jit(solution)/shard_map/convert
  233.7 0.8 copy-done.1
  234.5 1.0 dynamic-slice_convert_fusion.3
  236.2 9.0 %cosine_convert_fusion.2 = (bf16[512,1024]{1,0:T(8,128)(2,1)S(1)}, bf16[512,1024]{1,0:T(8,128)(2,1)S(1)}) fusion(s32[1024]{0:T(1024)S(1)} %iota_add_fusion.4, s32[512]{0:T(512)S(1)} %iota_add_fusion.5), kind=kLoop, calls=%fused_computation.17.clone.1 | loop fusion | flops 8912896 | bytes 2103296 | tf_op jit(solution)/shard_map/convert
  245.8 0.8 copy-done.1
  246.6 1.0 dynamic-slice_convert_fusion.3
  248.3 9.0 %cosine_convert_fusion.2 = (bf16[512,1024]{1,0:T(8,128)(2,1)S(1)}, bf16[512,1024]{1,0:T(8,128)(2,1)S(1)}) fusion(s32[1024]{0:T(1024)S(1)} %iota_add_fusion.4, s32[512]{0:T(512)S(1)} %iota_add_fusion.5), kind=kLoop, calls=%fused_computation.17.clone.1 | loop fusion | flops 8912896 | bytes 2103296 | tf_op jit(solution)/shard_map/convert
  257.9 0.8 copy-done.1
  258.7 1.0 dynamic-slice_convert_fusion.3
  260.4 9.0 %cosine_convert_fusion.2 = (bf16[512,1024]{1,0:T(8,128)(2,1)S(1)}, bf16[512,1024]{1,0:T(8,128)(2,1)S(1)}) fusion(s32[1024]{0:T(1024)S(1)} %iota_add_fusion.4, s32[512]{0:T(512)S(1)} %iota_add_fusion.5), kind=kLoop, calls=%fused_computation.17.clone.1 | loop fusion | flops 8912896 | bytes 2103296 | tf_op jit(solution)/shard_map/convert
  270.1 0.8 copy-done.1
  270.9 1.0 dynamic-slice_convert_fusion.3
  272.5 9.0 %cosine_convert_fusion.2 = (bf16[512,1024]{1,0:T(8,128)(2,1)S(1)}, bf16[512,1024]{1,0:T(8,128)(2,1)S(1)}) fusion(s32[1024]{0:T(1024)S(1)} %iota_add_fusion.4, s32[512]{0:T(512)S(1)} %iota_add_fusion.5), kind=kLoop, calls=%fused_computation.17.clone.1 | loop fusion | flops 8912896 | bytes 2103296 | tf_op jit(solution)/shard_map/convert
  282.2 0.8 copy-done.1
  283.0 1.0 dynamic-slice_convert_fusion.3
  284.6 9.0 %cosine_convert_fusion.2 = (bf16[512,1024]{1,0:T(8,128)(2,1)S(1)}, bf16[512,1024]{1,0:T(8,128)(2,1)S(1)}) fusion(s32[1024]{0:T(1024)S(1)} %iota_add_fusion.4, s32[512]{0:T(512)S(1)} %iota_add_fusion.5), kind=kLoop, calls=%fused_computation.17.clone.1 | loop fusion | flops 8912896 | bytes 2103296 | tf_op jit(solution)/shard_map/convert
  294.3 0.8 copy-done.1
  295.1 1.0 dynamic-slice_convert_fusion.3
  296.8 9.0 %cosine_convert_fusion.2 = (bf16[512,1024]{1,0:T(8,128)(2,1)S(1)}, bf16[512,1024]{1,0:T(8,128)(2,1)S(1)}) fusion(s32[1024]{0:T(1024)S(1)} %iota_add_fusion.4, s32[512]{0:T(512)S(1)} %iota_add_fusion.5), kind=kLoop, calls=%fused_computation.17.clone.1 | loop fusion | flops 8912896 | bytes 2103296 | tf_op jit(solution)/shard_map/convert
  306.4 0.8 copy-done.1
  307.2 1.0 dynamic-slice_convert_fusion.3
  308.9 9.0 %cosine_convert_fusion.2 = (bf16[512,1024]{1,0:T(8,128)(2,1)S(1)}, bf16[512,1024]{1,0:T(8,128)(2,1)S(1)}) fusion(s32[1024]{0:T(1024)S(1)} %iota_add_fusion.4, s32[512]{0:T(512)S(1)} %iota_add_fusion.5), kind=kLoop, calls=%fused_computation.17.clone.1 | loop fusion | flops 8912896 | bytes 2103296 | tf_op jit(solution)/shard_map/convert
  318.5 0.8 copy-done.1
  319.3 1.0 dynamic-slice_convert_fusion.3
  321.0 9.0 %cosine_convert_fusion.2 = (bf16[512,1024]{1,0:T(8,128)(2,1)S(1)}, bf16[512,1024]{1,0:T(8,128)(2,1)S(1)}) fusion(s32[1024]{0:T(1024)S(1)} %iota_add_fusion.4, s32[512]{0:T(512)S(1)} %iota_add_fusion.5), kind=kLoop, calls=%fused_computation.17.clone.1 | loop fusion | flops 8912896 | bytes 2103296 | tf_op jit(solution)/shard_map/convert
  330.6 0.8 copy-done.1
  331.4 1.0 dynamic-slice_convert_fusion.3
  333.1 9.0 %cosine_convert_fusion.2 = (bf16[512,1024]{1,0:T(8,128)(2,1)S(1)}, bf16[512,1024]{1,0:T(8,128)(2,1)S(1)}) fusion(s32[1024]{0:T(1024)S(1)} %iota_add_fusion.4, s32[512]{0:T(512)S(1)} %iota_add_fusion.5), kind=kLoop, calls=%fused_computation.17.clone.1 | loop fusion | flops 8912896 | bytes 2103296 | tf_op jit(solution)/shard_map/convert
  342.8 0.8 copy-done.1
  343.6 1.0 dynamic-slice_convert_fusion.3
  345.2 9.0 %cosine_convert_fusion.2 = (bf16[512,1024]{1,0:T(8,128)(2,1)S(1)}, bf16[512,1024]{1,0:T(8,128)(2,1)S(1)}) fusion(s32[1024]{0:T(1024)S(1)} %iota_add_fusion.4, s32[512]{0:T(512)S(1)} %iota_add_fusion.5), kind=kLoop, calls=%fused_computation.17.clone.1 | loop fusion | flops 8912896 | bytes 2103296 | tf_op jit(solution)/shard_map/convert
  354.9 0.8 copy-done.1
  355.7 1.0 dynamic-slice_convert_fusion.3
  357.3 9.0 %cosine_convert_fusion.2 = (bf16[512,1024]{1,0:T(8,128)(2,1)S(1)}, bf16[512,1024]{1,0:T(8,128)(2,1)S(1)}) fusion(s32[1024]{0:T(1024)S(1)} %iota_add_fusion.4, s32[512]{0:T(512)S(1)} %iota_add_fusion.5), kind=kLoop, calls=%fused_computation.17.clone.1 | loop fusion | flops 8912896 | bytes 2103296 | tf_op jit(solution)/shard_map/convert
  367.0 0.8 copy-done.1
  367.8 1.0 dynamic-slice_convert_fusion.3
  369.5 9.0 %cosine_convert_fusion.2 = (bf16[512,1024]{1,0:T(8,128)(2,1)S(1)}, bf16[512,1024]{1,0:T(8,128)(2,1)S(1)}) fusion(s32[1024]{0:T(1024)S(1)} %iota_add_fusion.4, s32[512]{0:T(512)S(1)} %iota_add_fusion.5), kind=kLoop, calls=%fused_computation.17.clone.1 | loop fusion | flops 8912896 | bytes 2103296 | tf_op jit(solution)/shard_map/convert
  379.1 0.8 copy-done.1
  379.9 1.0 dynamic-slice_convert_fusion.3
  381.6 9.0 %cosine_convert_fusion.2 = (bf16[512,1024]{1,0:T(8,128)(2,1)S(1)}, bf16[512,1024]{1,0:T(8,128)(2,1)S(1)}) fusion(s32[1024]{0:T(1024)S(1)} %iota_add_fusion.4, s32[512]{0:T(512)S(1)} %iota_add_fusion.5), kind=kLoop, calls=%fused_computation.17.clone.1 | loop fusion | flops 8912896 | bytes 2103296 | tf_op jit(solution)/shard_map/convert
  391.2 0.8 copy-done.1
  392.0 1.2 reshape.149
  393.2 1.2 copy.14
  394.4 38.7 %all-gather.5.cloned.1.call-done = f32[4,16,9,1024]{3,1,2,0:T(8,128)} async-done(((f32[1,16,9,1024]{3,1,2,0:T(8,128)}), f32[4,16,9,1024]{3,1,2,0:T(8,128)}) %all-gather.5.cloned.1.call-update) | async-done | bytes 2359312 | tf_op jit(solution)/shard_map/all_gather | solution.py:76
  433.2 1.9 reduce_sum.26
  435.1 0.9 multiply_multiply_fusion
  (195 shorter events, 19.1 us)
Async XLA Ops:
  6.5 2.4 copy-start.2
  6.5 3.4 copy-start.3
  6.5 156.3 %all-gather.3.cloned.1.call-start = ((), (), s32[]{:S(2)}) async-start(), calls=%async_computation | async-start | bytes 13369344 | tf_op jit(solution)/shard_map/all_gather | solution.py:56
  7.3 425.9 %all-gather.5.cloned.1.call-start = ((), (), s32[]{:S(2)}) async-start(), calls=%async_computation.1 | async-start | bytes 2949120 | tf_op jit(solution)/shard_map/all_gather | solution.py:76
  199.2 9.6 %copy-start = (f32[144,1024]{1,0:T(8,128)S(1)}, f32[144,1024]{1,0:T(8,128)}, u32[]{:S(2)}) copy-start(f32[144,1024]{1,0:T(8,128)} %get-tuple-element.211) | copy-start | bytes 1769476 | tf_op jit(solution)/shard_map/while
  209.4 0.8 copy-start.1
  211.4 9.6 %copy-start = (f32[144,1024]{1,0:T(8,128)S(1)}, f32[144,1024]{1,0:T(8,128)}, u32[]{:S(2)}) copy-start(f32[144,1024]{1,0:T(8,128)} %get-tuple-element.211) | copy-start | bytes 1769476 | tf_op jit(solution)/shard_map/while
  221.6 0.8 copy-start.1
  223.5 9.6 %copy-start = (f32[144,1024]{1,0:T(8,128)S(1)}, f32[144,1024]{1,0:T(8,128)}, u32[]{:S(2)}) copy-start(f32[144,1024]{1,0:T(8,128)} %get-tuple-element.211) | copy-start | bytes 1769476 | tf_op jit(solution)/shard_map/while
  233.7 0.8 copy-start.1
  235.6 9.6 %copy-start = (f32[144,1024]{1,0:T(8,128)S(1)}, f32[144,1024]{1,0:T(8,128)}, u32[]{:S(2)}) copy-start(f32[144,1024]{1,0:T(8,128)} %get-tuple-element.211) | copy-start | bytes 1769476 | tf_op jit(solution)/shard_map/while
  245.8 0.8 copy-start.1
  247.7 9.6 %copy-start = (f32[144,1024]{1,0:T(8,128)S(1)}, f32[144,1024]{1,0:T(8,128)}, u32[]{:S(2)}) copy-start(f32[144,1024]{1,0:T(8,128)} %get-tuple-element.211) | copy-start | bytes 1769476 | tf_op jit(solution)/shard_map/while
  257.9 0.8 copy-start.1
  259.8 9.6 %copy-start = (f32[144,1024]{1,0:T(8,128)S(1)}, f32[144,1024]{1,0:T(8,128)}, u32[]{:S(2)}) copy-start(f32[144,1024]{1,0:T(8,128)} %get-tuple-element.211) | copy-start | bytes 1769476 | tf_op jit(solution)/shard_map/while
  270.0 0.8 copy-start.1
  271.9 9.6 %copy-start = (f32[144,1024]{1,0:T(8,128)S(1)}, f32[144,1024]{1,0:T(8,128)}, u32[]{:S(2)}) copy-start(f32[144,1024]{1,0:T(8,128)} %get-tuple-element.211) | copy-start | bytes 1769476 | tf_op jit(solution)/shard_map/while
  282.2 0.8 copy-start.1
  284.1 9.6 %copy-start = (f32[144,1024]{1,0:T(8,128)S(1)}, f32[144,1024]{1,0:T(8,128)}, u32[]{:S(2)}) copy-start(f32[144,1024]{1,0:T(8,128)} %get-tuple-element.211) | copy-start | bytes 1769476 | tf_op jit(solution)/shard_map/while
  294.3 0.8 copy-start.1
  296.2 9.6 %copy-start = (f32[144,1024]{1,0:T(8,128)S(1)}, f32[144,1024]{1,0:T(8,128)}, u32[]{:S(2)}) copy-start(f32[144,1024]{1,0:T(8,128)} %get-tuple-element.211) | copy-start | bytes 1769476 | tf_op jit(solution)/shard_map/while
  306.4 0.8 copy-start.1
  308.3 9.6 %copy-start = (f32[144,1024]{1,0:T(8,128)S(1)}, f32[144,1024]{1,0:T(8,128)}, u32[]{:S(2)}) copy-start(f32[144,1024]{1,0:T(8,128)} %get-tuple-element.211) | copy-start | bytes 1769476 | tf_op jit(solution)/shard_map/while
  318.5 0.8 copy-start.1
  320.4 9.6 %copy-start = (f32[144,1024]{1,0:T(8,128)S(1)}, f32[144,1024]{1,0:T(8,128)}, u32[]{:S(2)}) copy-start(f32[144,1024]{1,0:T(8,128)} %get-tuple-element.211) | copy-start | bytes 1769476 | tf_op jit(solution)/shard_map/while
  330.6 0.8 copy-start.1
  332.5 9.6 %copy-start = (f32[144,1024]{1,0:T(8,128)S(1)}, f32[144,1024]{1,0:T(8,128)}, u32[]{:S(2)}) copy-start(f32[144,1024]{1,0:T(8,128)} %get-tuple-element.211) | copy-start | bytes 1769476 | tf_op jit(solution)/shard_map/while
  342.7 0.8 copy-start.1
  344.7 9.6 %copy-start = (f32[144,1024]{1,0:T(8,128)S(1)}, f32[144,1024]{1,0:T(8,128)}, u32[]{:S(2)}) copy-start(f32[144,1024]{1,0:T(8,128)} %get-tuple-element.211) | copy-start | bytes 1769476 | tf_op jit(solution)/shard_map/while
  354.9 0.8 copy-start.1
  356.8 9.6 %copy-start = (f32[144,1024]{1,0:T(8,128)S(1)}, f32[144,1024]{1,0:T(8,128)}, u32[]{:S(2)}) copy-start(f32[144,1024]{1,0:T(8,128)} %get-tuple-element.211) | copy-start | bytes 1769476 | tf_op jit(solution)/shard_map/while
  367.0 0.8 copy-start.1
  368.9 9.6 %copy-start = (f32[144,1024]{1,0:T(8,128)S(1)}, f32[144,1024]{1,0:T(8,128)}, u32[]{:S(2)}) copy-start(f32[144,1024]{1,0:T(8,128)} %get-tuple-element.211) | copy-start | bytes 1769476 | tf_op jit(solution)/shard_map/while
  379.1 0.8 copy-start.1
  381.0 9.6 %copy-start = (f32[144,1024]{1,0:T(8,128)S(1)}, f32[144,1024]{1,0:T(8,128)}, u32[]{:S(2)}) copy-start(f32[144,1024]{1,0:T(8,128)} %get-tuple-element.211) | copy-start | bytes 1769476 | tf_op jit(solution)/shard_map/while
  391.2 0.8 copy-start.1
Sparse Core Ops, SparseCore 0:
  9.4 153.3 all-gather.2
  394.5 38.6 all-gather.4
